TPU v7x, 256 devices: a whole 4x4x8 slice. The times are simulated.
256 devices in a mesh: row: 32 (over z, x), col: 8 (over y, core).
Axes of the slice: x: 4, y: 4, z: 8, core: 2. Of those that a mesh axis runs over, the one named last changes fastest.
Arguments:
- right_side: float32 [15, 512, 512], P(None, 'row'), may hold values from -6 to 6
- off_blocks: float32 [8, 512, 2176], P('col', 'row'), may hold values from -0.09375 to 0.09375
- diag_inverse: float32 [8, 512, 960], P('col', 'row'), as said below
Outputs:
- forward_solution: float32 [8, 960, 512], P('col')
- solution: float32 [8, 4, 512, 512], P('col', None, 'row')
Inputs may be any that keep to these rules, and one draw needn't show every extreme that they name: `diag_inverse`: read through the block map of the first step, each block D(n) is lower triangular with a positive diagonal between 0.5 and 2.
All inputs are finite; a program needn't handle non-finite values.
Results may differ from a plain program's by a relative error of at most 0.00011.
Values sent between devices are 32-bit elements; how exact they have to be, the bound alone decides.
No kernel may reach another device: no remote copies, remote signals or barrier semaphores. Data moves between devices by JAX's collectives and lax.ppermute only.
A program may use at most 64 MiB of HBM per device.

v0:
```python
import jax
import jax.numpy as jnp
from jax import lax
from jax.sharding import PartitionSpec as P

W = 512
LEVELS = 4


def swapped(value, axis, apart):
    mask = 2**apart
    pairs = [(source, source ^ mask) for source in range(lax.axis_size(axis))]
    return lax.ppermute(value, axis, pairs)


def pair_start(depth_down, depth_up):
    return (depth_down - 2) * 2**depth_down + 2 + depth_up * 2**depth_down


def group_sum(values, bit_count):
    for bit_num in range(bit_count):
        values = values + swapped(values, "col", bit_num)
    return values


def solve_block(right_side, off_blocks, diag_inverse):
    highest = lax.Precision.HIGHEST
    col_count = lax.axis_size("col")
    column = lax.axis_index("col")
    totals = [None] * LEVELS
    forward = [None] * LEVELS
    for depth_now in reversed(range(LEVELS)):
        group = col_count >> depth_now
        width = W // group
        bit_count = group.bit_length() - 1
        node_index = 2**depth_now - 1 + column // group
        residue = lax.dynamic_index_in_dim(right_side, node_index, 0, keepdims=False)
        if totals[depth_now] is not None:
            residue = residue - group_sum(totals[depth_now], bit_count)
        start = (2**depth_now - 1) * W // col_count
        inverse = diag_inverse[0, :, start : start + width]
        partial_value = jnp.einsum(
            "ba,br->ar", inverse, residue, precision=highest, preferred_element_type=jnp.float32
        )
        solved = lax.psum(partial_value, "row")
        forward[depth_now] = solved
        for depth_up in range(depth_now):
            begin = pair_start(depth_now, depth_up) * W // col_count
            block = off_blocks[0, :, begin : begin + width]
            term = jnp.dot(block, solved, precision=highest, preferred_element_type=jnp.float32)
            totals[depth_up] = term if totals[depth_up] is None else totals[depth_up] + term
    totals_down = [None] * LEVELS
    backward = [None] * LEVELS
    for depth_now in range(LEVELS):
        group = col_count >> depth_now
        width = W // group
        bit_count = group.bit_length() - 1
        residue = forward[depth_now]
        if totals_down[depth_now] is not None:
            residue = residue - lax.psum(totals_down[depth_now], "row")
        start = (2**depth_now - 1) * W // col_count
        inverse = diag_inverse[0, :, start : start + width]
        partial_value = jnp.dot(
            inverse, residue, precision=highest, preferred_element_type=jnp.float32
        )
        solved = group_sum(partial_value, bit_count)
        backward[depth_now] = solved
        for depth_down in range(depth_now + 1, LEVELS):
            width_down = W // (col_count >> depth_down)
            begin = pair_start(depth_down, depth_now) * W // col_count
            block = off_blocks[0, :, begin : begin + width_down]
            term = jnp.einsum(
                "ij,ir->jr", block, solved, precision=highest, preferred_element_type=jnp.float32
            )
            totals_down[depth_down] = (
                term if totals_down[depth_down] is None else totals_down[depth_down] + term
            )
    return (jnp.concatenate(forward, axis=0)[None], jnp.stack(backward, axis=0)[None])


def per_device(right_side, off_blocks, diag_inverse):
    forward_piece, backward_piece = solve_block(right_side, off_blocks, diag_inverse)
    return (forward_piece, backward_piece)


def solution(mesh):
    return jax.shard_map(
        per_device,
        mesh=mesh,
        in_specs=(P(None, "row", None), P("col", "row", None), P("col", "row", None)),
        out_specs=(P("col", None, None), P("col", None, "row", None)),
        check_vma=False,
    )
```

profile of v0, /device:TPU:8, one launch (start us, length us, event | category | flops | bytes accessed | tf_op | source)
XLA Modules:
  0.0 1091.3 jit_solution(8329834675328494492)
XLA Ops:
  7.2 0.0 all-reduce.8.cloned.1.call-start
  7.2 2.9 convolution_bitcast_fusion
  10.1 0.0 all-reduce.8.cloned.1.call-update
  10.1 0.0 all-reduce.10.cloned.1.call-start
  10.2 154.2 %all-reduce.8.cloned.1.call-done = f32[512,512]{0,1:T(8,128)} async-done(((f32[512,512]{0,1:T(8,128)}), f32[512,512]{0,1:T(8,128)}) %all-reduce.8.cloned.1.call-update) | async-done | bytes 1048592 | tf_op jit(solution)/shard_map/psum | solution.py:45
  164.3 2.3 convolution_bitcast_fusion.8
  166.6 0.1 collective-permute-start
  166.7 1.2 collective-permute-done
  167.9 2.2 convolution_bitcast_fusion.1
  170.1 0.0 all-reduce.10.cloned.1.call-update
  170.1 0.0 all-reduce.12.cloned.1.call-start
  170.2 144.9 %all-reduce.10.cloned.1.call-done = f32[256,512]{0,1:T(8,128)} async-done(((f32[256,512]{0,1:T(8,128)}), f32[256,512]{0,1:T(8,128)}) %all-reduce.10.cloned.1.call-update) | async-done | bytes 524304 | tf_op jit(solution)/shard_map/psum | solution.py:45
  315.1 1.7 fusion.36
  316.8 1.0 fusion.4
  317.8 0.1 collective-permute-start.1
  317.8 1.2 collective-permute-done.1
  319.0 0.5 collective-permute-start.2
  319.6 3.4 collective-permute-done.2
  323.0 2.1 convolution_bitcast_fusion.4
  325.1 0.0 all-reduce.14.cloned.1.call-start
  325.1 0.5 fusion.39
  325.7 1.0 convolution_add_fusion.4
  326.7 139.5 %all-reduce.12.cloned.1.call-done = f32[128,512]{0,1:T(8,128)} async-done(((f32[128,512]{0,1:T(8,128)}), f32[128,512]{0,1:T(8,128)}) %all-reduce.12.cloned.1.call-update) | async-done | bytes 262160 | tf_op jit(solution)/shard_map/psum | solution.py:45
  466.2 1.4 fusion.3
  467.5 0.1 collective-permute-start.3
  467.6 1.2 collective-permute-done.3
  468.8 0.5 collective-permute-start.4
  469.4 3.4 collective-permute-done.4
  472.8 2.1 collective-permute-start.5
  474.9 3.3 collective-permute-done.5
  478.2 2.1 convolution_bitcast_fusion.3
  480.3 0.0 all-reduce.16.cloned.1.call-start
  480.3 141.1 %all-reduce.14.cloned.1.call-done = f32[64,512]{0,1:T(8,128)} async-done(((f32[64,512]{0,1:T(8,128)}), f32[64,512]{0,1:T(8,128)}) %all-reduce.14.cloned.1.call-update) | async-done | bytes 131088 | tf_op jit(solution)/shard_map/psum | solution.py:45
  621.5 1.3 convolution_bitcast_fusion.7
  622.7 0.1 collective-permute-start.6
  622.8 1.2 collective-permute-done.6
  624.0 0.5 collective-permute-start.7
  624.6 3.4 collective-permute-done.7
  628.0 2.1 collective-permute-start.8
  630.1 3.3 collective-permute-done.8
  633.4 1.3 convolution_bitcast_fusion.2
  634.7 0.2 all-reduce.18.cloned.1.call-start
  634.9 141.0 %all-reduce.16.cloned.1.call-done = f32[128,512]{0,1:T(8,128)} async-done(((f32[128,512]{0,1:T(8,128)}), f32[128,512]{0,1:T(8,128)}) %all-reduce.16.cloned.1.call-update) | async-done | bytes 262160 | tf_op jit(solution)/shard_map/psum | solution.py:60
  775.9 1.3 convolution_bitcast_fusion.6
  777.2 0.1 collective-permute-start.9
  777.3 1.2 collective-permute-done.9
  778.5 0.5 collective-permute-start.10
  779.0 3.4 collective-permute-done.10
  782.4 0.6 fusion.34
  783.0 1.4 fusion.2
  784.5 0.0 all-reduce.20.cloned.1.call-start
  784.5 144.5 %all-reduce.18.cloned.1.call-done = f32[256,512]{0,1:T(8,128)} async-done(((f32[256,512]{0,1:T(8,128)}), f32[256,512]{0,1:T(8,128)}) %all-reduce.18.cloned.1.call-update) | async-done | bytes 524304 | tf_op jit(solution)/shard_map/psum | solution.py:60
  929.0 1.6 convolution_bitcast_fusion.9
  930.6 0.1 collective-permute-start.11
  930.7 1.0 fusion.8
  931.7 0.2 collective-permute-done.11
  931.9 1.0 fusion.11
  932.9 2.0 fusion.1
  935.0 0.0 all-reduce.20.cloned.1.call-update
  935.0 1.8 maximum_bitcast_fusion
  936.9 1.8 copy.6
  938.7 142.9 %all-reduce.20.cloned.1.call-done = f32[512,512]{0,1:T(8,128)} async-done(((f32[512,512]{0,1:T(8,128)}), f32[512,512]{0,1:T(8,128)}) %all-reduce.20.cloned.1.call-update) | async-done | bytes 1048592 | tf_op jit(solution)/shard_map/psum | solution.py:60
  1081.6 2.2 convolution_bitcast_fusion.5
  1083.8 0.7 maximum_bitcast_fusion.1
  (29 shorter events, 0.2 us)
Async XLA Ops:
  7.2 160.7 %copy-start.4 = (f32[1,16,960]{2,1,0:T(8,128)S(1)}, f32[1,16,960]{2,1,0:T(8,128)}, u32[]{:S(2)}) copy-start(f32[1,16,960]{2,1,0:T(8,128)} %param.5) | copy-start | bytes 184324
  7.2 157.2 %copy-start.3 = (f32[1,16,2176]{2,1,0:T(8,128)S(1)}, f32[1,16,2176]{2,1,0:T(8,128)}, u32[]{:S(2)}) copy-start(f32[1,16,2176]{2,1,0:T(8,128)} %param.4) | copy-start | bytes 417796
  7.2 157.1 %all-reduce.8.cloned.1.call-start = ((), (), s32[]{:S(2)}) async-start(), calls=%async_computation | async-start | bytes 2097152 | tf_op jit(solution)/shard_map/psum | solution.py:45
  10.1 305.0 %all-reduce.10.cloned.1.call-start = ((), (), s32[]{:S(2)}) async-start(), calls=%async_computation.1 | async-start | bytes 1048576 | tf_op jit(solution)/shard_map/psum | solution.py:45
  164.3 152.4 %copy-start = (f32[512,512]{0,1:T(8,128)S(1)}, f32[512,512]{0,1:T(8,128)}, u32[]{:S(2)}) copy-start(f32[512,512]{0,1:T(8,128)} %all-reduce.8.cloned.1.call-done) | copy-start | bytes 3145732
  166.6 1.3 collective-permute-start
  170.1 296.1 %all-reduce.12.cloned.1.call-start = ((), (), s32[]{:S(2)}) async-start(), calls=%async_computation.2 | async-start | bytes 524288 | tf_op jit(solution)/shard_map/psum | solution.py:45
  315.1 10.0 copy-start.1
  317.8 1.3 collective-permute-start.1
  319.0 3.9 collective-permute-start.2
  325.1 296.4 %all-reduce.14.cloned.1.call-start = ((), (), s32[]{:S(2)}) async-start(), calls=%async_computation.3 | async-start | bytes 524288 | tf_op jit(solution)/shard_map/psum | solution.py:45
  466.2 309.7 %copy-start.2 = (f32[128,512]{0,1:T(8,128)S(1)}, f32[128,512]{0,1:T(8,128)}, u32[]{:S(2)}) copy-start(f32[128,512]{0,1:T(8,128)} %all-reduce.12.cloned.1.call-done) | copy-start | bytes 786436
  467.5 1.3 collective-permute-start.3
  468.8 3.9 collective-permute-start.4
  472.8 5.4 collective-permute-start.5
  480.3 295.6 %all-reduce.16.cloned.1.call-start = ((), (), s32[]{:S(2)}) async-start(), calls=%async_computation.4 | async-start | bytes 524288 | tf_op jit(solution)/shard_map/psum | solution.py:60
  622.7 1.3 collective-permute-start.6
  624.0 3.9 collective-permute-start.7
  628.0 5.4 collective-permute-start.8
  634.7 294.3 %all-reduce.18.cloned.1.call-start = ((), (), s32[]{:S(2)}) async-start(), calls=%async_computation.5 | async-start | bytes 1048576 | tf_op jit(solution)/shard_map/psum | solution.py:60
  777.2 1.3 collective-permute-start.9
  778.5 3.9 collective-permute-start.10
  784.5 297.1 %all-reduce.20.cloned.1.call-start = ((), (), s32[]{:S(2)}) async-start(), calls=%async_computation.6 | async-start | bytes 2097152 | tf_op jit(solution)/shard_map/psum | solution.py:60
  930.6 1.3 collective-permute-start.11
  931.9 3.1 copy-start.6
  936.9 1.8 copy-start.7
  936.9 144.7 %copy-start.5 = (f32[1,16,960]{2,1,0:T(8,128)S(1)}, f32[1,16,960]{2,1,0:T(8,128)}, u32[]{:S(2)}) copy-start(f32[1,16,960]{2,1,0:T(8,128)} %param.5) | copy-start | bytes 184324
Sparse Core Ops, SparseCore 0:
  12.0 152.2 all-reduce.7
  170.2 144.8 all-reduce.9
  325.2 140.9 all-reduce.11
  480.4 141.0 all-reduce.13
  634.8 141.0 all-reduce.15
  784.6 144.4 all-reduce.17
  935.1 146.3 all-reduce.19
where the time goes:
time: 1090 us
  waiting for transfers between devices  1030 us (94%)
  matrix products  30.9 us (3%)
  between operations  14.3 us (1%)
    psum x4, waiting for transfers between devices, solve_block(): solved = lax.psum(partial_value, 'row')  580 us
    psum x3, waiting for transfers between devices, solve_block(): residue = residue - lax.psum(totals_down[depth_now], 'row')  428 us
    ppermute x12, waiting for transfers between devices, swapped(): return lax.ppermute(value, axis, pairs)  26.2 us
  transfers between devices with their start and end apart: 19, of which 19 were waited for; matrix products, arithmetic and copies ran while one was open for 1% of the time, Pallas kernels for 0%

commit v1 on v0

--- a/solution.py
+++ b/solution.py
@@ -42,7 +42,9 @@
         partial_value = jnp.einsum(
             "ba,br->ar", inverse, residue, precision=highest, preferred_element_type=jnp.float32
         )
-        solved = lax.psum(partial_value, "row")
+        solved = partial_value
+        for hop in (1, 2, 4, 8, 16):
+            solved = solved + lax.ppermute(solved, "row", [(dev, dev ^ hop) for dev in range(32)])
         forward[depth_now] = solved
         for depth_up in range(depth_now):
             begin = pair_start(depth_now, depth_up) * W // col_count

time: 1090 us -> 855 us (0.78)
  waiting for transfers between devices: 1030 us -> 770 us
  starting transfers between devices: 7.32 us -> 45.8 us
    psum x4 -> x0, waiting for transfers between devices: 580 us -> none  [solve_block(): solved = lax.psum(partial_value, 'row')]
    ppermute x0 -> x20, waiting for transfers between devices: none -> 309 us  [solve_block(): lax.ppermute(solved, 'row', [(dev, dev ^ hop) for dev in range(32)])]
    ppermute x0 -> x20, starting transfers between devices: none -> 40 us  [solve_block(): lax.ppermute(solved, 'row', [(dev, dev ^ hop) for dev in range(32)])]
  transfers between devices with their start and end apart: 19 -> 35, of which waited for: 19 -> 35; matrix products, arithmetic and copies ran while one was open for 1% -> 0% of each run, Pallas kernels for 0% -> 0%
where the time goes in v1:
time: 855 us; the launch traced here: 854 us
  waiting for transfers between devices  770 us (90%)
  starting transfers between devices  45.8 us (5%)
  matrix products  20.8 us (2%)
  between operations  14 us (2%)
    psum x3, waiting for transfers between devices, solve_block(): residue = residue - lax.psum(totals_down[depth_now], 'row')  433 us
    ppermute x20, waiting for transfers between devices, solve_block(): lax.ppermute(solved, 'row', [(dev, dev ^ hop) for dev in range(32)])  309 us
    ppermute x20, starting transfers between devices, solve_block(): lax.ppermute(solved, 'row', [(dev, dev ^ hop) for dev in range(32)])  40 us
    ppermute x12, waiting for transfers between devices, swapped(): return lax.ppermute(value, axis, pairs)  27.4 us
  transfers between devices with their start and end apart: 35, of which 35 were waited for; matrix products, arithmetic and copies ran while one was open for 0% of the time, Pallas kernels for 0%

profile of v1, /device:TPU:8, one launch (start us, length us, event | category | flops | bytes accessed | tf_op | source)
XLA Modules:
  0.0 854.5 jit_solution(12170131740878921339)
XLA Ops:
  7.2 1.9 convolution_bitcast_fusion
  9.1 1.6 collective-permute-start
  10.7 23.4 %collective-permute-done = f32[512,512]{1,0:T(8,128)S(1)} collective-permute-done((f32[512,512]{1,0:T(8,128)S(1)}, f32[512,512]{1,0:T(8,128)S(1)}, u32[]{:S(2)}, u32[]{:S(2)}) %collective-permute-start) | collective-permute-done | bytes 1048608 | tf_op jit(solution)/shard_map/ppermute | solution.py:47
  34.3 3.1 collective-permute-start.1
  37.5 22.5 %collective-permute-done.1 = f32[512,512]{1,0:T(8,128)S(1)} collective-permute-done((f32[512,512]{1,0:T(8,128)S(1)}, f32[512,512]{1,0:T(8,128)S(1)}, u32[]{:S(2)}, u32[]{:S(2)}) %collective-permute-start.1) | collective-permute-done | bytes 1048608 | tf_op jit(solution)/shard_map/ppermute | solution.py:47
  60.2 2.0 collective-permute-start.2
  62.2 21.4 %collective-permute-done.2 = f32[512,512]{1,0:T(8,128)S(1)} collective-permute-done((f32[512,512]{1,0:T(8,128)S(1)}, f32[512,512]{1,0:T(8,128)S(1)}, u32[]{:S(2)}, u32[]{:S(2)}) %collective-permute-start.2) | collective-permute-done | bytes 1048608 | tf_op jit(solution)/shard_map/ppermute | solution.py:47
  83.7 3.4 collective-permute-start.3
  87.1 43.1 %collective-permute-done.3 = f32[512,512]{1,0:T(8,128)S(1)} collective-permute-done((f32[512,512]{1,0:T(8,128)S(1)}, f32[512,512]{1,0:T(8,128)S(1)}, u32[]{:S(2)}, u32[]{:S(2)}) %collective-permute-start.3) | collective-permute-done | bytes 1048608 | tf_op jit(solution)/shard_map/ppermute | solution.py:47
  130.4 6.3 collective-permute-start.4
  136.7 45.7 %collective-permute-done.4 = f32[512,512]{1,0:T(8,128)S(1)} collective-permute-done((f32[512,512]{1,0:T(8,128)S(1)}, f32[512,512]{1,0:T(8,128)S(1)}, u32[]{:S(2)}, u32[]{:S(2)}) %collective-permute-start.4) | collective-permute-done | bytes 1048608 | tf_op jit(solution)/shard_map/ppermute | solution.py:47
  183.4 1.2 collective-permute-done.5
  184.6 1.4 convolution_bitcast_fusion.1
  186.0 1.6 collective-permute-start.6
  187.7 12.4 %collective-permute-done.6 = f32[256,512]{1,0:T(8,128)S(1)} collective-permute-done((f32[256,512]{1,0:T(8,128)S(1)}, f32[256,512]{1,0:T(8,128)S(1)}, u32[]{:S(2)}, u32[]{:S(2)}) %collective-permute-start.6) | collective-permute-done | bytes 524320 | tf_op jit(solution)/shard_map/ppermute | solution.py:47
  200.2 3.1 collective-permute-start.7
  203.3 11.7 %collective-permute-done.7 = f32[256,512]{1,0:T(8,128)S(1)} collective-permute-done((f32[256,512]{1,0:T(8,128)S(1)}, f32[256,512]{1,0:T(8,128)S(1)}, u32[]{:S(2)}, u32[]{:S(2)}) %collective-permute-start.7) | collective-permute-done | bytes 524320 | tf_op jit(solution)/shard_map/ppermute | solution.py:47
  215.1 12.2 %collective-permute-done.8 = f32[256,512]{1,0:T(8,128)S(1)} collective-permute-done((f32[256,512]{1,0:T(8,128)S(1)}, f32[256,512]{1,0:T(8,128)S(1)}, u32[]{:S(2)}, u32[]{:S(2)}) %collective-permute-start.8) | collective-permute-done | bytes 524320 | tf_op jit(solution)/shard_map/ppermute | solution.py:47
  227.4 1.9 collective-permute-start.9
  229.4 21.6 %collective-permute-done.9 = f32[256,512]{1,0:T(8,128)S(1)} collective-permute-done((f32[256,512]{1,0:T(8,128)S(1)}, f32[256,512]{1,0:T(8,128)S(1)}, u32[]{:S(2)}, u32[]{:S(2)}) %collective-permute-start.9) | collective-permute-done | bytes 524320 | tf_op jit(solution)/shard_map/ppermute | solution.py:47
  251.1 3.0 collective-permute-start.10
  254.1 25.6 %collective-permute-done.10 = f32[256,512]{1,0:T(8,128)S(1)} collective-permute-done((f32[256,512]{1,0:T(8,128)S(1)}, f32[256,512]{1,0:T(8,128)S(1)}, u32[]{:S(2)}, u32[]{:S(2)}) %collective-permute-start.10) | collective-permute-done | bytes 524320 | tf_op jit(solution)/shard_map/ppermute | solution.py:47
  280.9 1.2 collective-permute-done.11
  282.6 3.5 collective-permute-done.12
  286.0 1.2 convolution_bitcast_fusion.3
  287.3 1.8 collective-permute-start.13
  289.1 5.7 collective-permute-done.13
  294.8 3.0 collective-permute-start.14
  297.8 5.0 collective-permute-done.14
  302.9 7.1 collective-permute-done.15
  310.0 1.8 collective-permute-start.16
  311.8 8.2 collective-permute-done.16
  320.1 2.8 collective-permute-start.17
  323.3 11.8 %collective-permute-done.17 = f32[128,512]{1,0:T(8,128)S(1)} collective-permute-done((f32[128,512]{1,0:T(8,128)S(1)}, f32[128,512]{1,0:T(8,128)S(1)}, u32[]{:S(2)}, u32[]{:S(2)}) %collective-permute-start.17) | collective-permute-done | bytes 262176 | tf_op jit(solution)/shard_map/ppermute | solution.py:47
  336.1 1.2 collective-permute-done.18
  337.8 3.5 collective-permute-done.19
  341.2 1.9 collective-permute-start.20
  343.2 3.5 collective-permute-done.20
  346.7 1.1 convolution_bitcast_fusion.4
  347.7 1.6 collective-permute-start.21
  349.3 3.5 collective-permute-done.21
  352.8 2.5 collective-permute-start.22
  355.3 4.1 collective-permute-done.22
  359.5 5.7 collective-permute-done.23
  365.4 10.0 %collective-permute-done.24 = f32[64,512]{1,0:T(8,128)S(1)} collective-permute-done((f32[64,512]{1,0:T(8,128)S(1)}, f32[64,512]{1,0:T(8,128)S(1)}, u32[]{:S(2)}, u32[]{:S(2)}) %collective-permute-start.24) | collective-permute-done | bytes 131104 | tf_op jit(solution)/shard_map/ppermute | solution.py:47
  375.5 8.9 %collective-permute-done.25 = f32[64,512]{1,0:T(8,128)S(1)} collective-permute-done((f32[64,512]{1,0:T(8,128)S(1)}, f32[64,512]{1,0:T(8,128)S(1)}, u32[]{:S(2)}, u32[]{:S(2)}) %collective-permute-start.25) | collective-permute-done | bytes 131104 | tf_op jit(solution)/shard_map/ppermute | solution.py:47
  384.7 1.2 collective-permute-done.26
  386.0 3.8 collective-permute-done.27
  389.8 1.7 collective-permute-start.28
  391.5 3.7 collective-permute-done.28
  395.2 1.1 convolution_bitcast_fusion.2
  396.4 143.4 %all-reduce.4.cloned.1.call-done = f32[128,512]{1,0:T(8,128)} async-done(((f32[128,512]{1,0:T(8,128)}), f32[128,512]{1,0:T(8,128)}) %all-reduce.4.cloned.1.call-update) | async-done | bytes 262160 | tf_op jit(solution)/shard_map/psum | solution.py:62
  539.9 1.2 convolution_bitcast_fusion.6
  541.2 1.2 collective-permute-done.29
  543.0 3.4 collective-permute-done.30
  546.9 1.4 fusion.2
  548.4 144.5 %all-reduce.6.cloned.1.call-done = f32[256,512]{1,0:T(8,128)} async-done(((f32[256,512]{1,0:T(8,128)}), f32[256,512]{1,0:T(8,128)}) %all-reduce.6.cloned.1.call-update) | async-done | bytes 524304 | tf_op jit(solution)/shard_map/psum | solution.py:62
  693.0 1.5 convolution_bitcast_fusion.9
  694.6 1.0 fusion.9
  695.8 1.0 fusion.12
  696.8 2.1 fusion.1
  698.9 1.4 maximum_bitcast_fusion
  700.3 145.1 %all-reduce.8.cloned.1.call-done = f32[512,512]{1,0:T(8,128)} async-done(((f32[512,512]{1,0:T(8,128)}), f32[512,512]{1,0:T(8,128)}) %all-reduce.8.cloned.1.call-update) | async-done | bytes 1048592 | tf_op jit(solution)/shard_map/psum | solution.py:62
  845.4 1.9 convolution_bitcast_fusion.5
  (64 shorter events, 9.1 us)
Async XLA Ops:
  7.2 532.7 %all-reduce.4.cloned.1.call-start = ((), (), s32[]{:S(2)}) async-start(), calls=%async_computation | async-start | bytes 524288 | tf_op jit(solution)/shard_map/psum | solution.py:62
  9.1 25.0 %collective-permute-start = (f32[512,512]{1,0:T(8,128)S(1)}, f32[512,512]{1,0:T(8,128)S(1)}, u32[]{:S(2)}, u32[]{:S(2)}) collective-permute-start(f32[512,512]{1,0:T(8,128)S(1)} %convolution_bitcast_fusion), channel_id=1, source_target_pairs={{0,8},{8,0},{16,24},{24,16},{32,40},{40,32},{48,56},{56,48},{64,72... | collective-permute-start | bytes 3145736 | tf_op jit(solution)/shard_map/ppermute | solution.py:47
  34.3 25.6 %collective-permute-start.1 = (f32[512,512]{1,0:T(8,128)S(1)}, f32[512,512]{1,0:T(8,128)S(1)}, u32[]{:S(2)}, u32[]{:S(2)}) collective-permute-start(f32[512,512]{1,0:T(8,128)S(1)} %add.162), channel_id=1, source_target_pairs={{0,16},{8,24},{16,0},{24,8},{32,48},{40,56},{48,32},{56,40},{64,80... | collective-permute-start | bytes 3145736 | tf_op jit(solution)/shard_map/ppermute | solution.py:47
  60.2 23.4 %collective-permute-start.2 = (f32[512,512]{1,0:T(8,128)S(1)}, f32[512,512]{1,0:T(8,128)S(1)}, u32[]{:S(2)}, u32[]{:S(2)}) collective-permute-start(f32[512,512]{1,0:T(8,128)S(1)} %add.163), channel_id=1, source_target_pairs={{0,32},{8,40},{16,48},{24,56},{32,0},{40,8},{48,16},{56,24},{64,96... | collective-permute-start | bytes 3145736 | tf_op jit(solution)/shard_map/ppermute | solution.py:47
  83.7 46.4 %collective-permute-start.3 = (f32[512,512]{1,0:T(8,128)S(1)}, f32[512,512]{1,0:T(8,128)S(1)}, u32[]{:S(2)}, u32[]{:S(2)}) collective-permute-start(f32[512,512]{1,0:T(8,128)S(1)} %add.164), channel_id=1, source_target_pairs={{0,64},{8,72},{16,80},{24,88},{32,96},{40,104},{48,112},{56,120},{... | collective-permute-start | bytes 3145736 | tf_op jit(solution)/shard_map/ppermute | solution.py:47
  130.4 52.3 %copy-start = (f32[1,16,2176]{2,1,0:T(8,128)S(1)}, f32[1,16,2176]{2,1,0:T(8,128)}, u32[]{:S(2)}) copy-start(f32[1,16,2176]{2,1,0:T(8,128)} %param.4) | copy-start | bytes 417796
  130.4 54.2 %copy-start.1 = (f32[1,16,960]{2,1,0:T(8,128)S(1)}, f32[1,16,960]{2,1,0:T(8,128)}, u32[]{:S(2)}) copy-start(f32[1,16,960]{2,1,0:T(8,128)} %param.5) | copy-start | bytes 184324
  130.4 52.1 %collective-permute-start.4 = (f32[512,512]{1,0:T(8,128)S(1)}, f32[512,512]{1,0:T(8,128)S(1)}, u32[]{:S(2)}, u32[]{:S(2)}) collective-permute-start(f32[512,512]{1,0:T(8,128)S(1)} %add.165), channel_id=1, source_target_pairs={{0,128},{8,136},{16,144},{24,152},{32,160},{40,168},{48,176},{56,1... | collective-permute-start | bytes 3145736 | tf_op jit(solution)/shard_map/ppermute | solution.py:47
  183.3 1.3 collective-permute-start.5
  186.0 14.1 %collective-permute-start.6 = (f32[256,512]{1,0:T(8,128)S(1)}, f32[256,512]{1,0:T(8,128)S(1)}, u32[]{:S(2)}, u32[]{:S(2)}) collective-permute-start(f32[256,512]{1,0:T(8,128)S(1)} %convolution_bitcast_fusion.1), channel_id=1, source_target_pairs={{0,8},{8,0},{16,24},{24,16},{32,40},{40,32},{48,56},{56,48},{64,72... | collective-permute-start | bytes 1572872 | tf_op jit(solution)/shard_map/ppermute | solution.py:47
  200.2 14.8 %collective-permute-start.7 = (f32[256,512]{1,0:T(8,128)S(1)}, f32[256,512]{1,0:T(8,128)S(1)}, u32[]{:S(2)}, u32[]{:S(2)}) collective-permute-start(f32[256,512]{1,0:T(8,128)S(1)} %add.169), channel_id=1, source_target_pairs={{0,16},{8,24},{16,0},{24,8},{32,48},{40,56},{48,32},{56,40},{64,80... | collective-permute-start | bytes 1572872 | tf_op jit(solution)/shard_map/ppermute | solution.py:47
  215.0 12.3 %collective-permute-start.8 = (f32[256,512]{1,0:T(8,128)S(1)}, f32[256,512]{1,0:T(8,128)S(1)}, u32[]{:S(2)}, u32[]{:S(2)}) collective-permute-start(f32[256,512]{1,0:T(8,128)S(1)} %add.170), channel_id=1, source_target_pairs={{0,32},{8,40},{16,48},{24,56},{32,0},{40,8},{48,16},{56,24},{64,96... | collective-permute-start | bytes 1572872 | tf_op jit(solution)/shard_map/ppermute | solution.py:47
  227.4 23.5 %collective-permute-start.9 = (f32[256,512]{1,0:T(8,128)S(1)}, f32[256,512]{1,0:T(8,128)S(1)}, u32[]{:S(2)}, u32[]{:S(2)}) collective-permute-start(f32[256,512]{1,0:T(8,128)S(1)} %add.171), channel_id=1, source_target_pairs={{0,64},{8,72},{16,80},{24,88},{32,96},{40,104},{48,112},{56,120},{... | collective-permute-start | bytes 1572872 | tf_op jit(solution)/shard_map/ppermute | solution.py:47
  251.1 28.6 %collective-permute-start.10 = (f32[256,512]{1,0:T(8,128)S(1)}, f32[256,512]{1,0:T(8,128)S(1)}, u32[]{:S(2)}, u32[]{:S(2)}) collective-permute-start(f32[256,512]{1,0:T(8,128)S(1)} %add.172), channel_id=1, source_target_pairs={{0,128},{8,136},{16,144},{24,152},{32,160},{40,168},{48,176},{56,1... | collective-permute-start | bytes 1572872 | tf_op jit(solution)/shard_map/ppermute | solution.py:47
  280.8 1.3 collective-permute-start.11
  282.1 3.9 collective-permute-start.12
  287.3 7.5 collective-permute-start.13
  294.8 8.0 collective-permute-start.14
  302.8 7.2 collective-permute-start.15
  310.0 10.0 %collective-permute-start.16 = (f32[128,512]{1,0:T(8,128)S(1)}, f32[128,512]{1,0:T(8,128)S(1)}, u32[]{:S(2)}, u32[]{:S(2)}) collective-permute-start(f32[128,512]{1,0:T(8,128)S(1)} %add.183), channel_id=1, source_target_pairs={{0,64},{8,72},{16,80},{24,88},{32,96},{40,104},{48,112},{56,120},{... | collective-permute-start | bytes 786440 | tf_op jit(solution)/shard_map/ppermute | solution.py:47
  320.1 15.0 %collective-permute-start.17 = (f32[128,512]{1,0:T(8,128)S(1)}, f32[128,512]{1,0:T(8,128)S(1)}, u32[]{:S(2)}, u32[]{:S(2)}) collective-permute-start(f32[128,512]{1,0:T(8,128)S(1)} %add.184), channel_id=1, source_target_pairs={{0,128},{8,136},{16,144},{24,152},{32,160},{40,168},{48,176},{56,1... | collective-permute-start | bytes 786440 | tf_op jit(solution)/shard_map/ppermute | solution.py:47
  336.0 1.3 collective-permute-start.18
  337.3 3.9 collective-permute-start.19
  341.2 5.4 collective-permute-start.20
  347.7 5.1 collective-permute-start.21
  352.8 6.6 collective-permute-start.22
  359.4 5.8 collective-permute-start.23
  365.2 10.2 %collective-permute-start.24 = (f32[64,512]{1,0:T(8,128)S(1)}, f32[64,512]{1,0:T(8,128)S(1)}, u32[]{:S(2)}, u32[]{:S(2)}) collective-permute-start(f32[64,512]{1,0:T(8,128)S(1)} %add.193), channel_id=1, source_target_pairs={{0,64},{8,72},{16,80},{24,88},{32,96},{40,104},{48,112},{56,120},{... | collective-permute-start | bytes 393224 | tf_op jit(solution)/shard_map/ppermute | solution.py:47
  375.4 9.0 %collective-permute-start.25 = (f32[64,512]{1,0:T(8,128)S(1)}, f32[64,512]{1,0:T(8,128)S(1)}, u32[]{:S(2)}, u32[]{:S(2)}) collective-permute-start(f32[64,512]{1,0:T(8,128)S(1)} %add.194), channel_id=1, source_target_pairs={{0,128},{8,136},{16,144},{24,152},{32,160},{40,168},{48,176},{56,1... | collective-permute-start | bytes 393224 | tf_op jit(solution)/shard_map/ppermute | solution.py:47
  384.6 1.3 collective-permute-start.26
  385.9 3.9 collective-permute-start.27
  389.8 5.4 collective-permute-start.28
  396.4 296.6 %all-reduce.6.cloned.1.call-start = ((), (), s32[]{:S(2)}) async-start(), calls=%async_computation.1 | async-start | bytes 1048576 | tf_op jit(solution)/shard_map/psum | solution.py:62
  541.1 1.3 collective-permute-start.29
  542.4 3.9 collective-permute-start.30
  548.4 297.0 %all-reduce.8.cloned.1.call-start = ((), (), s32[]{:S(2)}) async-start(), calls=%async_computation.2 | async-start | bytes 2097152 | tf_op jit(solution)/shard_map/psum | solution.py:62
  694.5 1.3 collective-permute-start.31
Sparse Core Ops, SparseCore 0:
  396.5 143.3 all-reduce.3
  548.5 144.4 all-reduce.5
  699.0 146.3 all-reduce.7
